TPU v7x, 256 devices: a whole 4x4x8 slice. The times are simulated.
256 devices in a mesh: env: 4 (over x_lo, core), tm: 64 (over x_hi, z, y).
Axes of the slice: x: 4 (x_hi: 2, x_lo: 2; x = x_hi * 2 + x_lo), y: 4, z: 8, core: 2. Of those that a mesh axis runs over, the one named last changes fastest.
Arguments:
- hidden: bfloat16 [4, 64, 256, 1024], P('env', 'tm'), may hold values from -6 to 6
- done_step: int32 [4, 64], P('env', 'tm'), may hold values from 0 to 255
- alive: int32 [4, 64, 256], P('env', None, 'tm'), may hold values 0 or 1
- targets: float32 [4, 64, 256], P('env', None, 'tm'), may hold values from -6 to 6
- gain_t: float32 [1024], replicated, may hold values from 0.25 to 1.75
- w_qkv_t: bfloat16 [1024, 3072], replicated, may hold values from -5 to 5
- w_out_t: bfloat16 [1024, 1024], replicated, may hold values from -0.1875 to 0.1875
- gain_a: float32 [1024], replicated, may hold values from 0.25 to 1.75
- w_qkv_a: bfloat16 [1024, 3072], P('tm'), may hold values from -5 to 5
- w_out_a: bfloat16 [1024, 1024], P('tm'), may hold values from -0.1875 to 0.1875
- w_value: float32 [1024], replicated, may hold values from -0.1875 to 0.1875
Outputs:
- values: float32 [4, 64, 256], P('env', None, 'tm')
- input_grad: bfloat16 [4, 64, 256, 1024], P('env', 'tm')
- qkv_grad: float32 [1024, 3072], P('tm')
- out_grad: float32 [1024, 1024], P('tm')
Inputs may be any that keep to these rules, and one draw needn't show every extreme that they name: `done_step`: the last step of an agent's first episode in the window; later steps form a new episode.
All inputs are finite; a program needn't handle non-finite values. No bound on the sum of `alive` on one device may be relied on, other than what follows from the above.
Results may differ from a plain program's by a relative error of at most 0.02.
Values may be sent and summed in bfloat16 or wider, within the bound.
A program may use at most 128 MiB of HBM per device.

v0:
```python
import math
import jax
import jax.numpy as jnp
from jax import lax
from jax.sharding import PartitionSpec as P

HEADS = 8


def norm_scale(rows, gain):
    return rows * lax.rsqrt(jnp.mean(rows * rows, axis=-1, keepdims=True) + 1e-06) * gain


def attend(qkv, allowed, head_count, layout):
    width = qkv.shape[-1] // 3
    size = width // head_count
    shape = qkv.shape[:-1] + (head_count, size)
    queries = qkv[..., :width].reshape(shape).astype(jnp.float32)
    key_rows = qkv[..., width : 2 * width].reshape(shape).astype(jnp.float32)
    value_rows = qkv[..., 2 * width :].reshape(shape).astype(jnp.float32)
    if layout == "temporal":
        score_form = "bqhe,bkhe->bhqk"
        mix_form = "bhqk,bkhe->bqhe"
    else:
        score_form = "qbhe,kbhe->bhqk"
        mix_form = "bhqk,kbhe->qbhe"
    scores = jnp.einsum(score_form, queries, key_rows) / math.sqrt(size)
    scores = jnp.where(allowed[:, None], scores, -1e30)
    row_max = jnp.max(scores, axis=-1, keepdims=True)
    weights = jnp.exp(scores - row_max)
    probs = (weights / jnp.sum(weights, axis=-1, keepdims=True)).astype(jnp.bfloat16)
    mixed = jnp.einsum(mix_form, probs.astype(jnp.float32), value_rows)
    return mixed.reshape(qkv.shape[:-1] + (width,))


def temporal_block(rows, done, gain, w_qkv, w_out, head_count):
    batch, length, width = rows.shape
    rows_f = rows.astype(jnp.float32)
    normed = norm_scale(rows_f, gain).astype(jnp.bfloat16)
    qkv = jnp.dot(normed.reshape(-1, width), w_qkv, preferred_element_type=jnp.float32)
    qkv = qkv.astype(jnp.bfloat16).reshape(batch, length, 3 * width)
    positions = jnp.arange(length, dtype=jnp.int32)
    later = positions[None, :] > done[:, None]
    causal = positions[:, None] >= positions[None, :]
    allowed = causal[None] & (later[:, :, None] == later[:, None, :])
    mixed = attend(qkv, allowed, head_count, "temporal").astype(jnp.bfloat16)
    added = jnp.dot(mixed.reshape(-1, width), w_out, preferred_element_type=jnp.float32)
    return (rows_f + added.reshape(batch, length, width)).astype(jnp.bfloat16)


def left_product(left, right):
    return lax.dot_general(
        left, right, (((0,), (0,)), ((), ())), preferred_element_type=jnp.float32
    )


def agent_step(lifted, alive_rows, target_rows, gain, w_qkv, w_out, w_value, head_count):
    agent_count, step_count, width = lifted.shape
    lifted_f = lifted.astype(jnp.float32)
    normed_f, norm_pull = jax.vjp(lambda rows: norm_scale(rows, gain), lifted_f)
    normed = normed_f.astype(jnp.bfloat16).reshape(-1, width)
    qkv = jnp.dot(normed, w_qkv, preferred_element_type=jnp.float32)
    qkv = qkv.astype(jnp.bfloat16).reshape(agent_count, step_count, 3 * width)
    living = alive_rows.T == 1
    allowed = living[:, None, :] | jnp.eye(agent_count, dtype=bool)[None]
    mixed_f, attend_pull = jax.vjp(lambda block: attend(block, allowed, head_count, "agents"), qkv)
    mixed = mixed_f.astype(jnp.bfloat16).reshape(-1, width)
    added = jnp.dot(mixed, w_out, preferred_element_type=jnp.float32)
    top_rows = lifted_f + added.reshape(agent_count, step_count, width)
    predicted = jnp.sum(top_rows * w_value, axis=-1)
    residual_err = 32.0 * alive_rows.astype(jnp.float32) * (predicted - target_rows)
    grad_top = residual_err[..., None] * w_value
    grad_rows = grad_top.astype(jnp.bfloat16).reshape(-1, width)
    grad_mixed = jnp.dot(grad_rows, w_out.T, preferred_element_type=jnp.float32)
    grad_qkv = attend_pull(grad_mixed.reshape(agent_count, step_count, width))[0]
    grad_qkv = grad_qkv.reshape(-1, 3 * width)
    grad_normed = jnp.dot(grad_qkv, w_qkv.T, preferred_element_type=jnp.float32)
    grad_lifted = grad_top + norm_pull(grad_normed.reshape(agent_count, step_count, width))[0]
    return (predicted, grad_lifted.astype(jnp.bfloat16), normed, grad_qkv, mixed, grad_rows)


def per_device(
    hidden, done_step, alive, targets, gain_t, w_qkv_t, w_out_t, gain_a, w_qkv_a, w_out_a, w_value
):
    width = hidden.shape[-1]
    local_rows = hidden[0]
    done_rows = done_step[0]
    first, pull = jax.vjp(
        lambda rows: temporal_block(rows, done_rows, gain_t, w_qkv_t, w_out_t, HEADS), local_rows
    )
    lifted = lax.all_to_all(first, "tm", split_axis=1, concat_axis=0, tiled=True)
    qkv_full, out_full = (
        lax.all_gather(w_qkv_a, "tm", axis=0, tiled=True),
        lax.all_gather(w_out_a, "tm", axis=0, tiled=True),
    )
    predicted, grad_lifted, normed, grad_qkv, mixed, grad_rows = agent_step(
        lifted, alive[0], targets[0], gain_a, qkv_full, out_full, w_value, HEADS
    )
    terms = jnp.concatenate(
        [left_product(normed, grad_qkv), left_product(mixed, grad_rows)], axis=1
    )
    summed = lax.psum_scatter(terms, "tm", scatter_dimension=0, tiled=True)
    totals = lax.psum(summed.astype(jnp.bfloat16), "env").astype(jnp.float32)
    qkv_grad = totals[:, : 3 * width]
    out_grad = totals[:, 3 * width :]
    returned = lax.all_to_all(grad_lifted, "tm", split_axis=0, concat_axis=1, tiled=True)
    input_grad = pull(returned)[0]
    return (predicted[None], input_grad[None], qkv_grad, out_grad)


def solution(mesh):
    in_specs = (
        P("env", "tm", None, None),
        P("env", "tm"),
        P("env", None, "tm"),
        P("env", None, "tm"),
        P(),
        P(),
        P(),
        P(),
        P("tm", None),
        P("tm", None),
        P(),
    )
    out_specs = (P("env", None, "tm"), P("env", "tm", None, None), P("tm", None), P("tm", None))
    return jax.shard_map(
        per_device, mesh=mesh, in_specs=in_specs, out_specs=out_specs, check_vma=False
    )
```

profile of v0, /device:TPU:1, one launch (start us, length us, event | category | flops | bytes accessed | tf_op | source)
XLA Modules:
  0.0 746.1 jit_solution(15809563214694229206)
XLA Ops:
  10.7 4.9 fusion.2
  24.9 5.6 reduce.17
  32.6 15.4 %all-to-all-start = ((bf16[64,2,2048]{2,1,0:T(2,128)(2,1)}), bf16[64,2,2048]{2,1,0:T(2,128)(2,1)}, u32[]{:S(2)}, u32[]{:S(2)}) async-start(bf16[64,2,2048]{2,1,0:T(2,128)(2,1)} %reshape.471), calls=%async_computation | async-start | bytes 1048576 | tf_op jit(solution)/shard_map/all_to_all | solution.py:91
  48.7 16.4 %all-to-all-done = bf16[64,2,2048]{2,1,0:T(2,128)(2,1)} async-done(((bf16[64,2,2048]{2,1,0:T(2,128)(2,1)}), bf16[64,2,2048]{2,1,0:T(2,128)(2,1)}, u32[]{:S(2)}, u32[]{:S(2)}) %all-to-all-start) | async-done | bytes 524320 | tf_op jit(solution)/shard_map/all_to_all | solution.py:91
  65.0 4.5 reshape.472
  69.5 6.9 multiply_reduce_fusion.1
  76.6 2.6 reshape.459
  79.1 3.3 bitcast_convert_fusion
  82.4 69.5 %all-gather.3.cloned.1.call-done = bf16[1024,3072]{1,0:T(8,128)(2,1)} async-done(((bf16[16,3072]{1,0:T(8,128)(2,1)}), bf16[1024,3072]{1,0:T(8,128)(2,1)}) %all-gather.3.cloned.1.call-update) | async-done | bytes 6291472 | tf_op jit(solution)/shard_map/all_gather | solution.py:93
  151.9 6.2 convolution_convert_fusion
  158.1 4.0 reshape.445
  162.1 2.9 fusion.129
  175.2 95.3 %all-gather.5.cloned.1.call-done = bf16[1024,1024]{1,0:T(8,128)(2,1)} async-done(((bf16[16,1024]{1,0:T(8,128)(2,1)}), bf16[1024,1024]{1,0:T(8,128)(2,1)}) %all-gather.5.cloned.1.call-update) | async-done | bytes 2097168 | tf_op jit(solution)/shard_map/all_gather | solution.py:94
  270.5 3.3 fusion.44
  282.0 3.5 multiply_reduce_fusion
  285.5 2.5 convolution_bitcast_fusion
  288.0 6.0 pad_maximum_fusion
  297.5 7.9 %all-to-all-start.1 = ((bf16[64,4,1024]{2,1,0:T(4,128)(2,1)}), bf16[64,4,1024]{2,1,0:T(4,128)(2,1)}, u32[]{:S(2)}, u32[]{:S(2)}) async-start(bf16[64,4,1024]{2,1,0:T(4,128)(2,1)} %copy.124), calls=%async_computation.1 | async-start | bytes 1048576 | tf_op jit(solution)/shard_map/all_to_all | solution.py:106
  305.5 19.2 %all-to-all-done.1 = bf16[64,4,1024]{2,1,0:T(4,128)(2,1)} async-done(((bf16[64,4,1024]{2,1,0:T(4,128)(2,1)}), bf16[64,4,1024]{2,1,0:T(4,128)(2,1)}, u32[]{:S(2)}, u32[]{:S(2)}) %all-to-all-start.1) | async-done | bytes 524320 | tf_op jit(solution)/shard_map/all_to_all | solution.py:106
  326.7 2.6 convolution_convert_fusion.5
  331.4 2.7 fusion.6
  339.1 2.9 fusion.58
  341.9 309.4 %reduce-scatter.2.cloned.1.call-done = f32[16,4096]{1,0:T(8,128)} async-done(((f32[1024,4096]{1,0:T(8,128)}), f32[16,4096]{1,0:T(8,128)}) %reduce-scatter.2.cloned.1.call-update) | async-done | bytes 262160 | tf_op jit(solution)/shard_map/reduce_scatter | solution.py:102
  655.4 81.0 %all-reduce.8.cloned.1.call-done = bf16[16,4096]{1,0:T(8,128)(2,1)} async-done(((bf16[16,4096]{1,0:T(8,128)(2,1)}), bf16[16,4096]{1,0:T(8,128)(2,1)}) %all-reduce.8.cloned.1.call-update) | async-done | bytes 131088 | tf_op jit(solution)/shard_map/psum | solution.py:103
  (130 shorter events, 52.6 us)
Async XLA Ops:
  7.2 14.6 %copy-start = (bf16[1024,1024]{1,0:T(8,128)(2,1)S(1)}, bf16[1024,1024]{1,0:T(8,128)(2,1)}, u32[]{:S(2)}) copy-start(bf16[1024,1024]{1,0:T(8,128)(2,1)} %param.17) | copy-start | bytes 6291460
  7.2 144.7 %all-gather.3.cloned.1.call-start = ((), (), s32[]{:S(2)}) async-start(), calls=%async_computation.3 | async-start | bytes 6389760 | tf_op jit(solution)/shard_map/all_gather | solution.py:93
  7.9 262.6 %all-gather.5.cloned.1.call-start = ((), (), s32[]{:S(2)}) async-start(), calls=%async_computation.4 | async-start | bytes 2129920 | tf_op jit(solution)/shard_map/all_gather | solution.py:94
  17.6 2.0 copy-start.10
  20.1 1.6 copy-start.5
  24.3 24.2 %copy-start.19 = (s32[1,64,4]{1,2,0:T(4,128)S(1)}, s32[1,64,4]{1,2,0:T(4,128)}, u32[]{:S(2)}) copy-start(s32[1,64,4]{1,2,0:T(4,128)} %param.13) | copy-start | bytes 3076
  32.6 32.4 %all-to-all-start = ((bf16[64,2,2048]{2,1,0:T(2,128)(2,1)}), bf16[64,2,2048]{2,1,0:T(2,128)(2,1)}, u32[]{:S(2)}, u32[]{:S(2)}) async-start(bf16[64,2,2048]{2,1,0:T(2,128)(2,1)} %reshape.471), calls=%async_computation | async-start | bytes 1048576 | tf_op jit(solution)/shard_map/all_to_all | solution.py:91
  48.0 603.4 %reduce-scatter.2.cloned.1.call-start = ((), (), s32[]{:S(2)}) async-start(), calls=%async_computation.5 | async-start | bytes 17039360 | tf_op jit(solution)/shard_map/reduce_scatter | solution.py:102
  76.6 75.3 %copy-start.24 = (f32[1024]{0:T(1024)S(1)}, f32[1024]{0:T(1024)}, u32[]{:S(2)}) copy-start(f32[1024]{0:T(1024)} %param.18) | copy-start | bytes 12292
  171.0 2.9 copy-start.15
  174.0 96.6 %copy-start.20 = (f32[1024]{0:T(1024)S(1)}, f32[1024]{0:T(1024)}, u32[]{:S(2)}) copy-start(f32[1024]{0:T(1024)} %param.21) | copy-start | bytes 12292
  175.2 98.6 %copy-start.21 = (f32[1,64,4]{1,2,0:T(4,128)S(1)}, f32[1,64,4]{1,2,0:T(4,128)}, u32[]{:S(2)}) copy-start(f32[1,64,4]{1,2,0:T(4,128)} %param.14) | copy-start | bytes 3076
  270.5 3.4 copy-start.23
  273.9 1.6 copy-start.22
  278.6 2.4 slice-start.2
  279.6 2.2 slice-start.3
  280.4 1.6 copy-start.9
  297.5 27.2 %all-to-all-start.1 = ((bf16[64,4,1024]{2,1,0:T(4,128)(2,1)}), bf16[64,4,1024]{2,1,0:T(4,128)(2,1)}, u32[]{:S(2)}, u32[]{:S(2)}) async-start(bf16[64,4,1024]{2,1,0:T(4,128)(2,1)} %copy.124), calls=%async_computation.1 | async-start | bytes 1048576 | tf_op jit(solution)/shard_map/all_to_all | solution.py:106
  305.4 430.9 %all-reduce.8.cloned.1.call-start = ((), (), s32[]{:S(2)}) async-start(), calls=%async_computation.6 | async-start | bytes 262144 | tf_op jit(solution)/shard_map/psum | solution.py:103
  331.4 2.7 copy-start.2
  335.6 2.4 slice-start
  336.9 2.2 slice-start.1
  336.9 2.2 copy-start.25
  339.1 313.9 %copy-start.14 = (bf16[256,1024]{1,0:T(8,128)(2,1)S(1)}, bf16[256,1024]{1,0:T(8,128)(2,1)}, u32[]{:S(2)}) copy-start(bf16[256,1024]{1,0:T(8,128)(2,1)} %all_to_all.8) | copy-start | bytes 1572868
  (13 other events, 15.4 us)
Sparse Core Ops, SparseCore 0:
  11.7 140.1 all-gather.2
  155.5 114.9 all-gather.4
  294.2 357.0 reduce-scatter.1
  654.4 81.9 all-reduce.7
where the time goes:
time: 755 us; the launch traced here: 746 us
  waiting for transfers between devices  592 us (78%)
  local copies, waits for them, and re-layouts  42.7 us (6%)
  matrix products  40 us (5%)
  other arithmetic  32.1 us (4%)
  starting transfers between devices  23.9 us (3%)
  between operations  15.2 us (2%)
    reduce_scatter x1, waiting for transfers between devices, per_device(): summed = lax.psum_scatter(terms, 'tm', scatter_dimension=0, tiled=True)  309 us
    all_gather x1, waiting for transfers between devices, per_device(): lax.all_gather(w_out_a, 'tm', axis=0, tiled=True)  95.3 us
    psum x1, waiting for transfers between devices, per_device(): totals = lax.psum(summed.astype(jnp.bfloat16), 'env').astype(jnp.float32)  81 us
    all_gather x1, waiting for transfers between devices, per_device(): lax.all_gather(w_qkv_a, 'tm', axis=0, tiled=True)  69.5 us
    all_to_all x1, waiting for transfers between devices, per_device(): lax.all_to_all(grad_lifted, 'tm', split_axis=0, concat_axis=1, tiled=True)  19.2 us
    all_to_all x1, waiting for transfers between devices, per_device(): lax.all_to_all(first, 'tm', split_axis=1, concat_axis=0, tiled=True)  16.4 us
    all_to_all x1, starting transfers between devices, per_device(): lax.all_to_all(first, 'tm', split_axis=1, concat_axis=0, tiled=True)  15.4 us
  transfers between devices with their start and end apart: 6, of which 6 were waited for; matrix products, arithmetic and copies ran while one was open for 11% of the time, Pallas kernels for 0%

commit v1 on v0

--- a/solution.py
+++ b/solution.py
@@ -5,6 +5,14 @@
 from jax.sharding import PartitionSpec as P
 
 HEADS = 8
+
+
+def place_skins(here_x, at_axis):
+    trail = []
+    for _ in range(lax.axis_size("tm")):
+        trail.append(here_x)
+    newest = jnp.concatenate(lax.all_to_all(jnp.stack(trail), "tm", 0, 0), axis=at_axis)
+    return newest
 
 
 def norm_scale(rows, gain):
@@ -91,7 +99,7 @@
     lifted = lax.all_to_all(first, "tm", split_axis=1, concat_axis=0, tiled=True)
     qkv_full, out_full = (
         lax.all_gather(w_qkv_a, "tm", axis=0, tiled=True),
-        lax.all_gather(w_out_a, "tm", axis=0, tiled=True),
+        place_skins(w_out_a, at_axis=0),
     )
     predicted, grad_lifted, normed, grad_qkv, mixed, grad_rows = agent_step(
         lifted, alive[0], targets[0], gain_a, qkv_full, out_full, w_value, HEADS

time: 755 us -> 679 us (0.90)
  waiting for transfers between devices: 592 us -> 488 us
  blocking collectives: 0 us -> 33.3 us
  starting transfers between devices: 23.9 us -> 15.3 us
    all_gather x1 -> x0, waiting for transfers between devices: 95.3 us -> none  [per_device(): lax.all_gather(w_out_a, 'tm', axis=0, tiled=True)]
    all_to_all x0 -> x1, blocking collectives: none -> 33.3 us  [per_device(): lax.all_to_all(first, 'tm', split_axis=1, concat_axis=0, tiled=True)]
    all_to_all x1, waiting for transfers between devices: 16.4 us -> 0.01 us  [place_skins(): lax.all_to_all(jnp.stack(trail), 'tm', 0, 0)]
    all_to_all x1, starting transfers between devices: 15.4 us -> 7.24 us  [place_skins(): lax.all_to_all(jnp.stack(trail), 'tm', 0, 0)]
  transfers between devices with their start and end apart: 6 -> 5, of which waited for: 6 -> 4; matrix products, arithmetic and copies ran while one was open for 11% -> 12% of each run, Pallas kernels for 0% -> 0%
where the time goes in v1:
time: 679 us; the launch traced here: 669 us
  waiting for transfers between devices  488 us (72%)
  local copies, waits for them, and re-layouts  43.6 us (6%)
  matrix products  41.6 us (6%)
  blocking collectives  33.3 us (5%)
  other arithmetic  32.1 us (5%)
  starting transfers between devices  15.3 us (2%)
  between operations  15.2 us (2%)
    reduce_scatter x1, waiting for transfers between devices, per_device(): summed = lax.psum_scatter(terms, 'tm', scatter_dimension=0, tiled=True)  310 us
    psum x1, waiting for transfers between devices, per_device(): totals = lax.psum(summed.astype(jnp.bfloat16), 'env').astype(jnp.float32)  80.4 us
    all_gather x1, waiting for transfers between devices, per_device(): lax.all_gather(w_qkv_a, 'tm', axis=0, tiled=True)  76.7 us
    all_to_all x1, blocking collectives, per_device(): lax.all_to_all(first, 'tm', split_axis=1, concat_axis=0, tiled=True)  33.3 us
    all_to_all x1, waiting for transfers between devices, per_device(): lax.all_to_all(grad_lifted, 'tm', split_axis=0, concat_axis=1, tiled=True)  20.7 us
    unnamed x67, local copies, waits for them, and re-layouts  14.4 us
  transfers between devices with their start and end apart: 5, of which 4 were waited for; matrix products, arithmetic and copies ran while one was open for 12% of the time, Pallas kernels for 0%

profile of v1, /device:TPU:1, one launch (start us, length us, event | category | flops | bytes accessed | tf_op | source)
XLA Modules:
  0.0 669.4 jit_solution(3363246298419904241)
XLA Ops:
  9.8 4.9 fusion.2
  24.0 5.6 reduce.17
  31.8 33.3 %all_to_all.26 = bf16[64,2,2048]{2,1,0:T(2,128)(2,1)} all-to-all(bf16[64,2,2048]{2,1,0:T(2,128)(2,1)} %reshape.479), channel_id=1, replica_groups=mesh['env'=4,'tm'=64] {'tm'}, dimensions={0} | all-to-all | bytes 1048576 | tf_op jit(solution)/shard_map/all_to_all | solution.py:99
  66.7 7.2 %all-to-all-start.1 = ((bf16[64,16,1024]{2,1,0:T(8,128)(2,1)}), bf16[64,16,1024]{2,1,0:T(8,128)(2,1)}, u32[]{:S(2)}, u32[]{:S(2)}) async-start(bf16[64,16,1024]{2,1,0:T(8,128)(2,1)} %stack.2), calls=%async_computation.1 | async-start | bytes 4194304 | tf_op jit(solution)/shard_map/all_to_all | solution.py:14
  74.6 4.4 reshape.480
  79.1 6.9 %multiply_reduce_fusion.1 = (f32[256]{0:T(256)S(1)}, f32[256,1024]{1,0:T(8,128)}) fusion(bf16[256,1,1024]{2,1,0:T(2,128)(2,1)} %reshape.480), kind=kLoop, calls=%fused_computation.92 | loop fusion | flops 786176 | bytes 1573888 | tf_op jit(solution)/shard_map/jvp()/reduce_sum | solution.py:19
  86.2 2.5 reshape.467
  88.8 3.3 bitcast_convert_fusion
  92.0 76.7 %all-gather.2.cloned.1.call-done = bf16[1024,3072]{1,0:T(8,128)(2,1)} async-done(((bf16[16,3072]{1,0:T(8,128)(2,1)}), bf16[1024,3072]{1,0:T(8,128)(2,1)}) %all-gather.2.cloned.1.call-update) | async-done | bytes 6291472 | tf_op jit(solution)/shard_map/all_gather | solution.py:101
  168.8 6.2 convolution_convert_fusion
  175.0 4.0 reshape.452
  179.0 2.9 fusion.120
  192.1 3.2 fusion.37
  195.3 2.4 convolution_bitcast_fusion.2
  204.6 3.5 multiply_reduce_fusion
  208.1 2.5 convolution_bitcast_fusion
  210.7 6.0 pad_maximum_fusion
  220.1 7.5 %all-to-all-start.2 = ((bf16[64,4,1024]{2,1,0:T(4,128)(2,1)}), bf16[64,4,1024]{2,1,0:T(4,128)(2,1)}, u32[]{:S(2)}, u32[]{:S(2)}) async-start(bf16[64,4,1024]{2,1,0:T(4,128)(2,1)} %copy.124), calls=%async_computation.2 | async-start | bytes 1048576 | tf_op jit(solution)/shard_map/all_to_all | solution.py:114
  227.7 20.7 %all-to-all-done.2 = bf16[64,4,1024]{2,1,0:T(4,128)(2,1)} async-done(((bf16[64,4,1024]{2,1,0:T(4,128)(2,1)}), bf16[64,4,1024]{2,1,0:T(4,128)(2,1)}, u32[]{:S(2)}, u32[]{:S(2)}) %all-to-all-start.2) | async-done | bytes 524320 | tf_op jit(solution)/shard_map/all_to_all | solution.py:114
  250.4 2.6 convolution_convert_fusion.5
  255.0 2.7 fusion.6
  262.7 2.9 fusion.49
  265.6 309.6 %reduce-scatter.2.cloned.1.call-done = f32[16,4096]{1,0:T(8,128)} async-done(((f32[1024,4096]{1,0:T(8,128)}), f32[16,4096]{1,0:T(8,128)}) %reduce-scatter.2.cloned.1.call-update) | async-done | bytes 262160 | tf_op jit(solution)/shard_map/reduce_scatter | solution.py:110
  579.2 80.4 %all-reduce.8.cloned.1.call-done = bf16[16,4096]{1,0:T(8,128)(2,1)} async-done(((bf16[16,4096]{1,0:T(8,128)(2,1)}), bf16[16,4096]{1,0:T(8,128)(2,1)}) %all-reduce.8.cloned.1.call-update) | async-done | bytes 131088 | tf_op jit(solution)/shard_map/psum | solution.py:111
  (129 shorter events, 52.1 us)
Async XLA Ops:
  7.2 13.8 %copy-start = (bf16[1024,1024]{1,0:T(8,128)(2,1)S(1)}, bf16[1024,1024]{1,0:T(8,128)(2,1)}, u32[]{:S(2)}) copy-start(bf16[1024,1024]{1,0:T(8,128)(2,1)} %param.17) | copy-start | bytes 6291460
  7.2 161.6 %all-gather.2.cloned.1.call-start = ((), (), s32[]{:S(2)}) async-start(), calls=%async_computation.4 | async-start | bytes 6389760 | tf_op jit(solution)/shard_map/all_gather | solution.py:101
  16.7 2.1 copy-start.10
  19.3 1.7 copy-start.5
  23.5 41.6 %copy-start.19 = (bf16[16,1024]{1,0:T(8,128)(2,1)S(1)}, bf16[16,1024]{1,0:T(8,128)(2,1)}, u32[]{:S(2)}) copy-start(bf16[16,1024]{1,0:T(8,128)(2,1)} %param.20) | copy-start | bytes 98308
  66.7 7.8 %copy-start.20 = (s32[1,64,4]{1,2,0:T(4,128)S(1)}, s32[1,64,4]{1,2,0:T(4,128)}, u32[]{:S(2)}) copy-start(s32[1,64,4]{1,2,0:T(4,128)} %param.13) | copy-start | bytes 3076
  66.7 125.3 %all-to-all-start.1 = ((bf16[64,16,1024]{2,1,0:T(8,128)(2,1)}), bf16[64,16,1024]{2,1,0:T(8,128)(2,1)}, u32[]{:S(2)}, u32[]{:S(2)}) async-start(bf16[64,16,1024]{2,1,0:T(8,128)(2,1)} %stack.2), calls=%async_computation.1 | async-start | bytes 4194304 | tf_op jit(solution)/shard_map/all_to_all | solution.py:14
  74.0 501.2 %reduce-scatter.2.cloned.1.call-start = ((), (), s32[]{:S(2)}) async-start(), calls=%async_computation.5 | async-start | bytes 17039360 | tf_op jit(solution)/shard_map/reduce_scatter | solution.py:110
  86.2 82.5 %copy-start.24 = (f32[1024]{0:T(1024)S(1)}, f32[1024]{0:T(1024)}, u32[]{:S(2)}) copy-start(f32[1024]{0:T(1024)} %param.18) | copy-start | bytes 12292
  188.0 2.8 copy-start.15
  192.1 3.2 copy-start.22
  195.3 2.8 copy-start.23
  195.3 2.5 copy-start.4
  201.2 2.4 slice-start.2
  202.2 2.2 slice-start.3
  203.0 1.6 copy-start.9
  220.1 28.3 %all-to-all-start.2 = ((bf16[64,4,1024]{2,1,0:T(4,128)(2,1)}), bf16[64,4,1024]{2,1,0:T(4,128)(2,1)}, u32[]{:S(2)}, u32[]{:S(2)}) async-start(bf16[64,4,1024]{2,1,0:T(4,128)(2,1)} %copy.124), calls=%async_computation.2 | async-start | bytes 1048576 | tf_op jit(solution)/shard_map/all_to_all | solution.py:114
  227.6 432.0 %all-reduce.8.cloned.1.call-start = ((), (), s32[]{:S(2)}) async-start(), calls=%async_computation.6 | async-start | bytes 262144 | tf_op jit(solution)/shard_map/psum | solution.py:111
  255.0 2.7 copy-start.2
  257.7 1.5 copy-start.11
  259.3 2.4 slice-start
  260.5 2.2 slice-start.1
  260.5 2.2 copy-start.25
  262.7 314.1 %copy-start.14 = (bf16[256,1024]{1,0:T(8,128)(2,1)S(1)}, bf16[256,1024]{1,0:T(8,128)(2,1)}, u32[]{:S(2)}) copy-start(bf16[256,1024]{1,0:T(8,128)(2,1)} %all_to_all.22) | copy-start | bytes 1572868
  (12 other events, 14.0 us)
Sparse Core Ops, SparseCore 0:
  11.7 156.9 all-gather.1
  216.8 358.2 reduce-scatter.1
  578.4 81.1 all-reduce.7
